TPU v7x, 32 devices: a whole 2x2x4 slice. The times are simulated.
32 devices in a mesh: groups: 1, patch: 32 (over z, y, x, core), level: 1.
Axes of the slice: x: 2, y: 2, z: 4, core: 2. Of those that a mesh axis runs over, the one named last changes fastest.
Arguments:
- layer_input: bfloat16 [1, 4096, 1536], P('groups', 'patch', 'level'), may hold values from -24 to 24, as said below
- cotangent: bfloat16 [1, 4096, 1536], P('groups', 'patch', 'level'), may hold values from -6 to 6
- neighbours: int32 [4096, 6], P('patch'), may hold values from 0 to 192, as said below
- boundary: int32 [32, 64], P('patch'), may hold values from 0 to 127, as said below
- gauge_index: int32 [4096, 6], P('patch'), may hold values from 0 to 1023
- gauge_angles: float32 [1024], replicated, may hold values from -3.140625 to 3.140625
- norm_gain: float32 [1536], replicated, may hold values from 0.5 to 1.5
- up_weight: bfloat16 [1536, 2048], P('patch', 'level'), may hold values from -0.15625 to 0.15625
- down_weight: bfloat16 [1536, 2048], P('patch', 'level'), may hold values from -0.125 to 0.125
- self_real: bfloat16 [32, 32], replicated, may hold values from -0.75 to 0.75
- self_imag: bfloat16 [32, 32], replicated, may hold values from -0.75 to 0.75
- near_real: bfloat16 [32, 32], replicated, may hold values from -1.5 to 1.5
- near_imag: bfloat16 [32, 32], replicated, may hold values from -1.5 to 1.5
Outputs:
- layer_grad: bfloat16 [1, 4096, 1536], P('groups', 'patch', 'level')
Inputs may be any that keep to these rules, and one draw needn't show every extreme that they name: `layer_input`: the layer input is a real field; rows and features carry differing scales. `neighbours`: entry i of a column's row refers to its patch's extended rows: i < 128 is the patch's own column i, then 32 boundary columns of the previous patch in the cycle, then 32 of the next one; 192 appears only in the last entry and marks an absent neighbour. `boundary`: row p holds 64 distinct local columns of patch p: the first 32 are seen by patch p - 1, the rest by patch p + 1 (patches form a cycle).
All inputs are finite; a program needn't handle non-finite values.
Results may differ from a plain program's by a relative error of at most 0.014.
Values may be sent and summed in bfloat16 or wider, within the bound.
No kernel may reach another device: no remote copies, remote signals or barrier semaphores. Data moves between devices by JAX's collectives and lax.ppermute only.
A program may use at most 64 MiB of HBM per device.

v0:
```python
import jax
import jax.numpy as jnp
from jax import lax
from jax.sharding import PartitionSpec as P

CH = 64


def padded(shard, sides, width):
    for axis, dim in sides:
        devices, length = (lax.axis_size(axis), shard.shape[dim])
        up = [(i, (i + 1) % devices) for i in range(devices)]
        down = [(j, i) for i, j in up]
        last = lax.slice_in_dim(shard, length - width, length, axis=dim)
        leading = lax.slice_in_dim(shard, 0, width, axis=dim)
        before = lax.ppermute(last, axis, up)
        after = lax.ppermute(leading, axis, down)
        shard = jnp.concatenate([before, shard, after], axis=dim)
    return shard


def real_form(real_part, imag_part):
    upper = jnp.concatenate([real_part, imag_part], axis=1)
    lower = jnp.concatenate([-imag_part, real_part], axis=1)
    return jnp.concatenate([upper, lower], axis=0)


def rotate_quarter(values, channels):
    shape = values.shape
    split = values.reshape(shape[:-1] + (shape[-1] // channels, 2, channels // 2))
    turned = jnp.stack([-split[..., 1, :], split[..., 0, :]], axis=-2)
    return turned.reshape(shape)


def per_level(values, form, channels):
    shape = values.shape
    split = values.reshape(shape[:-1] + (shape[-1] // channels, channels))
    result = jnp.einsum("bclw,wv->bclv", split, form, preferred_element_type=jnp.float32)
    return result.reshape(shape)


def mlp_back(columns_in, grads, norm_gain, up_mat, down_mat):
    values = columns_in.astype(jnp.float32)
    root_scale = lax.rsqrt(jnp.mean(values * values, axis=-1, keepdims=True) + 1e-05)
    normed = (values * root_scale * norm_gain).astype(jnp.bfloat16)
    pre_act = jnp.einsum("brw,wh->brh", normed, up_mat, preferred_element_type=jnp.float32)
    back_hidden = jnp.einsum("brw,wh->brh", grads, down_mat, preferred_element_type=jnp.float32)
    sigmoid_pre = jax.nn.sigmoid(pre_act)
    grad_pre = (back_hidden * sigmoid_pre * (1.0 + pre_act * (1.0 - sigmoid_pre))).astype(
        jnp.bfloat16
    )
    grad_normed = jnp.einsum("brh,wh->brw", grad_pre, up_mat, preferred_element_type=jnp.float32)
    mixed_mean = jnp.mean(norm_gain * grad_normed * values, axis=-1, keepdims=True)
    return (
        root_scale * norm_gain * grad_normed
        - values * root_scale * root_scale * root_scale * mixed_mean
    )


def per_device(
    layer_input,
    cotangent,
    neighbours,
    boundary,
    gauge_index,
    gauge_angles,
    norm_gain,
    up_weight,
    down_weight,
    self_real,
    self_imag,
    near_real,
    near_imag,
):
    samples, columns, width = layer_input.shape
    border = boundary.shape[1] // 2
    low_rows = boundary[0, :border]
    high_rows = boundary[0, border:]
    sent = jnp.stack([layer_input[:, low_rows], layer_input[:, high_rows]])
    cycle = padded(sent, (("patch", 0),), 1)
    extended = jnp.concatenate(
        [layer_input, cycle[0], cycle[3], jnp.zeros((samples, 1, width), jnp.bfloat16)], axis=1
    )
    sentinel = columns + 2 * border
    present = (neighbours < sentinel).astype(jnp.float32)
    edge_weight = present / jnp.sum(present, axis=1, keepdims=True)
    phase = gauge_angles[gauge_index]
    cosine = jnp.cos(phase)
    sine = jnp.sin(phase)
    near_form = real_form(near_real, near_imag)
    self_form = real_form(self_real, self_imag)
    gathered = jnp.zeros((samples, columns, width), jnp.float32)
    for entry in range(6):
        near = extended[:, neighbours[:, entry]].astype(jnp.float32)
        turned = rotate_quarter(near, CH)
        gathered = (
            gathered
            + (
                cosine[None, :, entry : entry + 1] * near
                + sine[None, :, entry : entry + 1] * turned
            )
            * edge_weight[None, :, entry : entry + 1]
        )
    gathered = gathered.astype(jnp.bfloat16)
    convolved = per_level(gathered, near_form, CH) + per_level(layer_input, self_form, CH)
    conv_out = (layer_input.astype(jnp.float32) + convolved).astype(jnp.bfloat16)
    conv_out = lax.optimization_barrier(conv_out)
    up_part, down_part = (
        lax.all_gather(up_weight, "patch", axis=0, tiled=True),
        lax.all_gather(down_weight, "patch", axis=0, tiled=True),
    )
    up_whole, down_whole = (
        lax.all_gather(up_part, "level", axis=1, tiled=True),
        lax.all_gather(down_part, "level", axis=1, tiled=True),
    )
    half_cols, half_grads = (
        lax.all_to_all(conv_out, "level", split_axis=1, concat_axis=2, tiled=True),
        lax.all_to_all(cotangent, "level", split_axis=1, concat_axis=2, tiled=True),
    )
    terms = mlp_back(half_cols, half_grads, norm_gain, up_whole, down_whole)
    column_grad = (half_grads.astype(jnp.float32) + terms).astype(jnp.bfloat16)
    grad_conv = lax.all_to_all(column_grad, "level", split_axis=2, concat_axis=1, tiled=True)
    grad_conv = lax.optimization_barrier(grad_conv)
    pulled = per_level(grad_conv, near_form.T, CH)
    own_back = per_level(grad_conv, self_form.T, CH)
    pulled_turn = rotate_quarter(pulled, CH)
    spread = jnp.zeros((samples, sentinel + 1, width), jnp.float32)
    for entry in range(6):
        edges = (
            cosine[None, :, entry : entry + 1] * pulled
            - sine[None, :, entry : entry + 1] * pulled_turn
        ) * edge_weight[None, :, entry : entry + 1]
        spread = spread.at[:, neighbours[:, entry]].add(edges)
    back_sent = jnp.stack(
        [spread[:, columns : columns + border], spread[:, columns + border : sentinel]]
    )
    back_cycle = padded(back_sent.astype(jnp.bfloat16), (("patch", 0),), 1).astype(back_sent.dtype)
    local_terms = (
        spread[:, :columns].at[:, low_rows].add(back_cycle[0]).at[:, high_rows].add(back_cycle[3])
    )
    return (grad_conv.astype(jnp.float32) + own_back + local_terms).astype(jnp.bfloat16)


def solution(mesh):
    in_specs = (
        P("groups", "patch", "level"),
        P("groups", "patch", "level"),
        P("patch", None),
        P("patch", None),
        P("patch", None),
        P(),
        P(),
        P("patch", "level"),
        P("patch", "level"),
        P(),
        P(),
        P(),
        P(),
    )
    out_specs = P("groups", "patch", "level")
    return jax.shard_map(
        per_device, mesh=mesh, in_specs=in_specs, out_specs=out_specs, check_vma=False
    )
```

profile of v0, /device:TPU:0, one launch (start us, length us, event | category | flops | bytes accessed | tf_op | source)
XLA Modules:
  0.0 208.6 jit_solution(11459584941339266616)
XLA Ops:
  8.8 1.8 gather_fusion.1
  11.8 6.0 %collective-permute-start.1 = (bf16[1,1,32,1536]{3,2,1,0:T(8,128)(2,1)S(1)}, bf16[1,1,32,1536]{3,2,1,0:T(8,128)(2,1)S(1)}, u32[]{:S(2)}, u32[]{:S(2)}) collective-permute-start(bf16[1,1,32,1536]{3,2,1,0:T(8,128)(2,1)S(1)} %bitcast.166), channel_id=1, source_target_pairs={{1,0},{2,1},{3,2},{4,3},{5,4},{6,5},{7,6},{8,7},{9,8},{10,9},{11,1... | collective-permute-start | bytes 294920 | tf_op jit(solution)/shard_map/ppermute | solution.py:17
  18.4 3.2 %gather_fusion = f32[768]{0:T(1024)S(1)} fusion(f32[1024]{0:T(1024)S(1)} %copy-done, s32[1024]{0:T(1024)S(1)} %pad_clamp_fusion.8), kind=kCustom, calls=%fused_computation | custom fusion | bytes 9216 | tf_op jit(solution)/shard_map/gather | solution.py:87
  29.5 1.6 gather_fusion.5
  32.3 1.6 gather_fusion.6
  34.0 2.1 copy.92
  36.0 1.6 gather_fusion.7
  37.7 2.1 copy.94
  39.7 1.6 gather_fusion.8
  41.4 2.1 copy.96
  50.0 32.1 %all-gather.5.cloned.1.call-done = bf16[1536,2048]{1,0:T(8,128)(2,1)} async-done(((bf16[48,2048]{1,0:T(8,128)(2,1)}), bf16[1536,2048]{1,0:T(8,128)(2,1)}) %all-gather.5.cloned.1.call-update) | async-done | bytes 6291472 | tf_op jit(solution)/shard_map/all_gather | solution.py:109
  82.1 3.8 %fusion.53 = f32[128,2048]{1,0:T(8,128)S(1)} fusion(bf16[1536,2048]{1,0:T(8,128)(2,1)} %all-gather.5.cloned.1.call-done, bf16[1,128,1536]{2,1,0:T(8,128)(2,1)S(1)} %add_convert_fusion, f32[1536]{0:T(1024)S(1)} %copy-done.19, f32[128]{0:T(128)S(1)} %add_rsqrt_fusion), kind=kOutput, calls=%fused_computation.87 | convolution fusion | flops 806092800 | bytes 7739904 | tf_op jit(solution)/shard_map/brw,wh->brh/dot_general | solution.py:46
  86.0 66.7 %all-gather.3.cloned.1.call-done = bf16[1536,2048]{1,0:T(8,128)(2,1)} async-done(((bf16[48,2048]{1,0:T(8,128)(2,1)}), bf16[1536,2048]{1,0:T(8,128)(2,1)}) %all-gather.3.cloned.1.call-update) | async-done | bytes 6291472 | tf_op jit(solution)/shard_map/all_gather | solution.py:110
  152.7 8.2 %fusion.11 = (f32[128]{0:T(128)S(1)}, f32[128,1536]{1,0:T(8,128)S(1)}) fusion(bf16[1,128,1536]{2,1,0:T(8,128)(2,1)S(1)} %add_convert_fusion, f32[1536]{0:T(1024)S(1)} %copy-done.19, bf16[1536,2048]{1,0:T(8,128)(2,1)} %all-gather.5.cloned.1.call-done, bf16[1536,2048]{1,0:T(8,128)(2,1)} %all-gather.3.cloned.1.call-done, f32[128,2048]{1,0:T(8,128)S(1)} %fusion.53, ...), kind=kOutput, calls=%fused_computation.34 | convolution fusion | flops 1613758336 | bytes 15211008 | tf_op jit(solution)/shard_map/brh,wh->brw/dot_general | solution.py:52
  163.3 3.4 %scatter_custom_fusion = f32[193,1536]{1,0:T(8,128)} fusion(s32[128]{0:T(128)} %copy-done.65, f32[1,128,1536]{2,1,0:T(8,128)S(1)} %copy.113, f32[1,128,1536]{2,1,0:T(8,128)S(1)} %copy.112, f32[]{:T(128)} %constant.5.clone.1, f32[128]{0:T(128)S(1)} %copy-done.28, f32[128]{0:T(128)S(1)} %get-tuple-element.11, f32[128]{0:T(128)S(1)} %copy-done.26), kind=kCustom, calls=%fused_computation.54 | custom fusion | flops 983040 | bytes 2760704 | tf_op jit(solution)/shard_map/scatter-add | solution.py:133
  166.7 4.4 %scatter_custom_fusion.1 = f32[193,1536]{1,0:T(8,128)} fusion(f32[193,1536]{1,0:T(8,128)} %scatter_custom_fusion, s32[128]{0:T(128)} %copy-done.64, f32[1,128,1536]{2,1,0:T(8,128)S(1)} %copy.113, f32[1,128,1536]{2,1,0:T(8,128)S(1)} %copy.112, f32[128]{0:T(128)S(1)} %copy-done.58, f32[128]{0:T(128)S(1)} %copy-done.46, f32[128]{0:T(128)S(1)} %copy-done.48), kind=kCustom, calls=%fused_computation.52 | custom fusion | flops 983040 | bytes 2760192 | tf_op jit(solution)/shard_map/scatter-add | solution.py:133
  171.2 4.4 %scatter_custom_fusion.2 = f32[193,1536]{1,0:T(8,128)} fusion(f32[193,1536]{1,0:T(8,128)} %scatter_custom_fusion.1, s32[128]{0:T(128)} %copy-done.63, f32[1,128,1536]{2,1,0:T(8,128)S(1)} %copy.113, f32[1,128,1536]{2,1,0:T(8,128)S(1)} %copy.112, f32[128]{0:T(128)S(1)} %copy-done.56, f32[128]{0:T(128)S(1)} %copy-done.42, f32[128]{0:T(128)S(1)} %copy-done.44), kind=kCustom, calls=%fused_computation.50 | custom fusion | flops 983040 | bytes 2760192 | tf_op jit(solution)/shard_map/scatter-add | solution.py:133
  175.6 4.4 %scatter_custom_fusion.3 = f32[193,1536]{1,0:T(8,128)} fusion(f32[193,1536]{1,0:T(8,128)} %scatter_custom_fusion.2, s32[128]{0:T(128)} %copy-done.62, f32[1,128,1536]{2,1,0:T(8,128)S(1)} %copy.113, f32[1,128,1536]{2,1,0:T(8,128)S(1)} %copy.112, f32[128]{0:T(128)S(1)} %copy-done.54, f32[128]{0:T(128)S(1)} %copy-done.38, f32[128]{0:T(128)S(1)} %copy-done.40), kind=kCustom, calls=%fused_computation.48 | custom fusion | flops 983040 | bytes 2760192 | tf_op jit(solution)/shard_map/scatter-add | solution.py:133
  180.1 4.4 %scatter_custom_fusion.4 = f32[193,1536]{1,0:T(8,128)} fusion(f32[193,1536]{1,0:T(8,128)} %scatter_custom_fusion.3, s32[128]{0:T(128)} %copy-done.61, f32[1,128,1536]{2,1,0:T(8,128)S(1)} %copy.113, f32[1,128,1536]{2,1,0:T(8,128)S(1)} %copy.112, f32[128]{0:T(128)S(1)} %copy-done.52, f32[128]{0:T(128)S(1)} %copy-done.34, f32[128]{0:T(128)S(1)} %copy-done.36), kind=kCustom, calls=%fused_computation.46 | custom fusion | flops 983040 | bytes 2760192 | tf_op jit(solution)/shard_map/scatter-add | solution.py:133
  184.5 4.4 %scatter_custom_fusion.5 = f32[193,1536]{1,0:T(8,128)} fusion(f32[193,1536]{1,0:T(8,128)} %scatter_custom_fusion.4, s32[128]{0:T(128)} %copy-done.60, f32[1,128,1536]{2,1,0:T(8,128)S(1)} %copy.113, f32[1,128,1536]{2,1,0:T(8,128)S(1)} %copy.112, f32[128]{0:T(128)S(1)} %copy-done.50, f32[128]{0:T(128)S(1)} %copy-done.30, f32[128]{0:T(128)S(1)} %copy-done.32), kind=kCustom, calls=%fused_computation.44 | custom fusion | flops 983040 | bytes 2760192 | tf_op jit(solution)/shard_map/scatter-add | solution.py:133
  190.8 5.1 %collective-permute-start.3 = (bf16[1,1,32,1536]{3,2,1,0:T(8,128)(2,1)S(1)}, bf16[1,1,32,1536]{3,2,1,0:T(8,128)(2,1)S(1)}, u32[]{:S(2)}, u32[]{:S(2)}) collective-permute-start(bf16[1,1,32,1536]{3,2,1,0:T(8,128)(2,1)S(1)} %bitcast.161), channel_id=1, source_target_pairs={{1,0},{2,1},{3,2},{4,3},{5,4},{6,5},{7,6},{8,7},{9,8},{10,9},{11,1... | collective-permute-start | bytes 294920 | tf_op jit(solution)/shard_map/ppermute | solution.py:17
  196.0 2.3 %collective-permute-done.2 = bf16[1,1,32,1536]{3,2,1,0:T(8,128)(2,1)S(1)} collective-permute-done((bf16[1,1,32,1536]{3,2,1,0:T(8,128)(2,1)S(1)}, bf16[1,1,32,1536]{3,2,1,0:T(8,128)(2,1)S(1)}, u32[]{:S(2)}, u32[]{:S(2)}) %collective-permute-start.2) | collective-permute-done | bytes 98336 | tf_op jit(solution)/shard_map/ppermute | solution.py:16
  198.2 1.3 scatter_custom_fusion.6
  199.6 1.4 scatter_custom_fusion.7
  (209 shorter events, 24.0 us)
Async XLA Ops:
  6.5 11.8 %copy-start = (f32[1024]{0:T(1024)S(1)}, f32[1024]{0:T(1024)}, u32[]{:S(2)}) copy-start(f32[1024]{0:T(1024)} %param.18) | copy-start | bytes 12292
  6.5 4.6 %copy-start.1 = (bf16[1,128,1536]{2,1,0:T(8,128)(2,1)S(1)}, bf16[1,128,1536]{2,1,0:T(8,128)(2,1)}, u32[]{:S(2)}) copy-start(bf16[1,128,1536]{2,1,0:T(8,128)(2,1)} %param.13) | copy-start | bytes 1179652
  6.5 75.6 %all-gather.5.cloned.1.call-start = ((), (), s32[]{:S(2)}) async-start(), calls=%async_computation.1 | async-start | bytes 6488064 | tf_op jit(solution)/shard_map/all_gather | solution.py:109
  7.3 145.4 %all-gather.3.cloned.1.call-start = ((), (), s32[]{:S(2)}) async-start(), calls=%async_computation | async-start | bytes 6488064 | tf_op jit(solution)/shard_map/all_gather | solution.py:110
  8.8 9.2 %copy-start.59 = (s32[128,6]{0,1:T(8,128)S(1)}, s32[128,6]{0,1:T(8,128)}, u32[]{:S(2)}) copy-start(s32[128,6]{0,1:T(8,128)} %param.17) | copy-start | bytes 9220
  10.6 16.5 %collective-permute-start = (bf16[1,1,32,1536]{3,2,1,0:T(8,128)(2,1)S(1)}, bf16[1,1,32,1536]{3,2,1,0:T(8,128)(2,1)S(1)}, u32[]{:S(2)}, u32[]{:S(2)}) collective-permute-start(bf16[1,1,32,1536]{3,2,1,0:T(8,128)(2,1)S(1)} %bitcast.164), channel_id=1, source_target_pairs={{0,1},{1,2},{2,3},{3,4},{4,5},{5,6},{6,7},{7,8},{8,9},{9,10},{10,1... | collective-permute-start | bytes 294920 | tf_op jit(solution)/shard_map/ppermute | solution.py:16
  11.8 15.3 %collective-permute-start.1 = (bf16[1,1,32,1536]{3,2,1,0:T(8,128)(2,1)S(1)}, bf16[1,1,32,1536]{3,2,1,0:T(8,128)(2,1)S(1)}, u32[]{:S(2)}, u32[]{:S(2)}) collective-permute-start(bf16[1,1,32,1536]{3,2,1,0:T(8,128)(2,1)S(1)} %bitcast.166), channel_id=1, source_target_pairs={{1,0},{2,1},{3,2},{4,3},{5,4},{6,5},{7,6},{8,7},{9,8},{10,9},{11,1... | collective-permute-start | bytes 294920 | tf_op jit(solution)/shard_map/ppermute | solution.py:17
  18.4 4.5 %copy-start.24 = (bf16[32,32]{1,0:T(8,128)(2,1)S(1)}, bf16[32,32]{1,0:T(8,128)(2,1)}, u32[]{:S(2)}) copy-start(bf16[32,32]{1,0:T(8,128)(2,1)} %param.24) | copy-start | bytes 6148
  18.4 5.2 %copy-start.20 = (s32[128,6]{0,1:T(8,128)S(1)}, s32[128,6]{0,1:T(8,128)}, u32[]{:S(2)}) copy-start(s32[128,6]{0,1:T(8,128)} %param.15) | copy-start | bytes 9220
  22.0 5.3 %copy-start.11 = (bf16[32,32]{0,1:T(8,128)(2,1)}, bf16[32,32]{0,1:T(8,128)(2,1)S(1)}, u32[]{:S(2)}) copy-start(bf16[32,32]{0,1:T(8,128)(2,1)S(1)} %neg.59) | copy-start | bytes 6148
  22.1 5.2 %copy-start.13 = (bf16[32,32]{0,1:T(8,128)(2,1)}, bf16[32,32]{0,1:T(8,128)(2,1)S(1)}, u32[]{:S(2)}) copy-start(bf16[32,32]{0,1:T(8,128)(2,1)S(1)} %copy.102) | copy-start | bytes 6148
  22.2 5.1 %copy-start.8 = (bf16[32,32]{0,1:T(8,128)(2,1)}, bf16[32,32]{0,1:T(8,128)(2,1)S(1)}, u32[]{:S(2)}) copy-start(bf16[32,32]{0,1:T(8,128)(2,1)S(1)} %copy.99) | copy-start | bytes 6148
  49.8 32.4 %copy-start.19 = (f32[1536]{0:T(1024)S(1)}, f32[1536]{0:T(1024)}, u32[]{:S(2)}) copy-start(f32[1536]{0:T(1024)} %param.19) | copy-start | bytes 18436
  50.0 102.7 %copy-start.7 = (bf16[1,128,1536]{2,1,0:T(8,128)(2,1)S(1)}, bf16[1,128,1536]{2,1,0:T(8,128)(2,1)}, u32[]{:S(2)}) copy-start(bf16[1,128,1536]{2,1,0:T(8,128)(2,1)} %param.14) | copy-start | bytes 1179652
  166.7 4.5 %copy-start.42 = (f32[128]{0:T(128)S(1)}, f32[128]{0:T(128)}, u32[]{:S(2)}) copy-start(f32[128]{0:T(128)} %get-tuple-element.15) | copy-start | bytes 1540
  166.7 4.4 %copy-start.44 = (f32[128]{0:T(128)S(1)}, f32[128]{0:T(128)}, u32[]{:S(2)}) copy-start(f32[128]{0:T(128)} %get-tuple-element.62) | copy-start | bytes 1540
  171.1 4.5 %copy-start.38 = (f32[128]{0:T(128)S(1)}, f32[128]{0:T(128)}, u32[]{:S(2)}) copy-start(f32[128]{0:T(128)} %get-tuple-element.14) | copy-start | bytes 1540
  171.2 4.4 %copy-start.40 = (f32[128]{0:T(128)S(1)}, f32[128]{0:T(128)}, u32[]{:S(2)}) copy-start(f32[128]{0:T(128)} %get-tuple-element.63) | copy-start | bytes 1540
  175.6 4.5 %copy-start.34 = (f32[128]{0:T(128)S(1)}, f32[128]{0:T(128)}, u32[]{:S(2)}) copy-start(f32[128]{0:T(128)} %get-tuple-element.13) | copy-start | bytes 1540
  175.6 4.4 %copy-start.36 = (f32[128]{0:T(128)S(1)}, f32[128]{0:T(128)}, u32[]{:S(2)}) copy-start(f32[128]{0:T(128)} %get-tuple-element.64) | copy-start | bytes 1540
  180.1 4.5 %copy-start.30 = (f32[128]{0:T(128)S(1)}, f32[128]{0:T(128)}, u32[]{:S(2)}) copy-start(f32[128]{0:T(128)} %get-tuple-element.12) | copy-start | bytes 1540
  180.1 4.4 %copy-start.32 = (f32[128]{0:T(128)S(1)}, f32[128]{0:T(128)}, u32[]{:S(2)}) copy-start(f32[128]{0:T(128)} %get-tuple-element.65) | copy-start | bytes 1540
  190.5 7.7 %collective-permute-start.2 = (bf16[1,1,32,1536]{3,2,1,0:T(8,128)(2,1)S(1)}, bf16[1,1,32,1536]{3,2,1,0:T(8,128)(2,1)S(1)}, u32[]{:S(2)}, u32[]{:S(2)}) collective-permute-start(bf16[1,1,32,1536]{3,2,1,0:T(8,128)(2,1)S(1)} %bitcast.162), channel_id=1, source_target_pairs={{0,1},{1,2},{2,3},{3,4},{4,5},{5,6},{6,7},{7,8},{8,9},{9,10},{10,1... | collective-permute-start | bytes 294920 | tf_op jit(solution)/shard_map/ppermute | solution.py:16
  190.8 7.4 %collective-permute-start.3 = (bf16[1,1,32,1536]{3,2,1,0:T(8,128)(2,1)S(1)}, bf16[1,1,32,1536]{3,2,1,0:T(8,128)(2,1)S(1)}, u32[]{:S(2)}, u32[]{:S(2)}) collective-permute-start(bf16[1,1,32,1536]{3,2,1,0:T(8,128)(2,1)S(1)} %bitcast.161), channel_id=1, source_target_pairs={{1,0},{2,1},{3,2},{4,3},{5,4},{6,5},{7,6},{8,7},{9,8},{10,9},{11,1... | collective-permute-start | bytes 294920 | tf_op jit(solution)/shard_map/ppermute | solution.py:17
  (50 other events, 91.1 us)
Sparse Core Ops, SparseCore 0:
  10.2 71.8 all-gather.4
  85.0 67.6 all-gather.2
where the time goes:
time: 209 us
  waiting for transfers between devices  103 us (49%)
  local copies, waits for them, and re-layouts  32.3 us (15%)
  other arithmetic  32.2 us (15%)
  matrix products  15.2 us (7%)
  between operations  14.4 us (7%)
  starting transfers between devices  12 us (6%)
    all_gather x1, waiting for transfers between devices, per_device(): lax.all_gather(down_weight, 'patch', axis=0, tiled=True)  66.7 us
    all_gather x1, waiting for transfers between devices, per_device(): lax.all_gather(up_weight, 'patch', axis=0, tiled=True)  32.1 us
    scatter-add x6, other arithmetic, per_device(): spread = spread.at[:, neighbours[:, entry]].add(edges)  25.5 us
    ppermute x2, starting transfers between devices, padded(): after = lax.ppermute(leading, axis, down)  11.1 us
    gather x6, local copies, waits for them, and re-layouts, per_device(): near = extended[:, neighbours[:, entry]].astype(jnp.float32)  8.36 us
    dot_general x1, matrix products, mlp_back(): jnp.einsum('brh,wh->brw', grad_pre, up_mat, preferred_element_type=jnp.fl...  8.23 us
    convert_element_type x6, local copies, waits for them, and re-layouts, per_device(): near = extended[:, neighbours[:, entry]].astype(jnp.float32)  7.69 us
    unnamed x141, local copies, waits for them, and re-layouts  5.98 us
  transfers between devices with their start and end apart: 6, of which 3 were waited for; matrix products, arithmetic and copies ran while one was open for 16% of the time, Pallas kernels for 0%

commit v1 on v0

--- a/solution.py
+++ b/solution.py
@@ -4,6 +4,18 @@
 from jax.sharding import PartitionSpec as P
 
 CH = 64
+
+
+def collect(x, axis, dim):
+    ways, here, step = (lax.axis_size(axis), lax.axis_index(axis), x.shape[dim])
+    line, have = (x, 1)
+    while have < ways:
+        line = jnp.concatenate(
+            [line, lax.ppermute(line, axis, [(d, (d - have) % ways) for d in range(ways)])],
+            axis=dim,
+        )
+        have = 2 * have
+    return jnp.roll(line, here * step, axis=dim)
 
 
 def padded(shard, sides, width):
@@ -107,7 +119,7 @@
     conv_out = lax.optimization_barrier(conv_out)
     up_part, down_part = (
         lax.all_gather(up_weight, "patch", axis=0, tiled=True),
-        lax.all_gather(down_weight, "patch", axis=0, tiled=True),
+        collect(down_weight, "patch", 0),
     )
     up_whole, down_whole = (
         lax.all_gather(up_part, "level", axis=1, tiled=True),

time: 209 us -> 344 us (1.65)
  waiting for transfers between devices: 103 us -> 191 us
  local copies, waits for them, and re-layouts: 32.3 us -> 55.1 us
  starting transfers between devices: 12 us -> 23 us
  other arithmetic: 32.2 us -> 39.3 us
  matrix products: 15.2 us -> 20 us
    ppermute x0 -> x5, waiting for transfers between devices: none -> 188 us  [collect(): lax.ppermute(line, axis, [(d, (d - have) % ways) for d in range(ways)])]
    all_gather x1 -> x0, waiting for transfers between devices: 66.7 us -> none  [per_device(): lax.all_gather(down_weight, 'patch', axis=0, tiled=True)]
    all_gather x1, waiting for transfers between devices: 32.1 us -> 0.01 us  [per_device(): lax.all_gather(up_weight, 'patch', axis=0, tiled=True)]
    unnamed x141 -> x165, local copies, waits for them, and re-layouts: 5.98 us -> 18.4 us
    concatenate x0 -> x2, local copies, waits for them, and re-layouts: none -> 7.57 us  [the longest x1 4.03 us: collect(): return jnp.roll(line, here * step, axis=dim)]
    ppermute x0 -> x5, starting transfers between devices: none -> 6.81 us  [collect(): lax.ppermute(line, axis, [(d, (d - have) % ways) for d in range(ways)])]
    ppermute x2, starting transfers between devices: 11.1 us -> 16.1 us  [padded(): after = lax.ppermute(leading, axis, down)]
  transfers between devices with their start and end apart: 6 -> 10, of which waited for: 3 -> 5; matrix products, arithmetic and copies ran while one was open for 16% -> 18% of each run, Pallas kernels for 0% -> 0%
where the time goes in v1:
time: 344 us; the launch traced here: 343 us
  waiting for transfers between devices  191 us (56%)
  local copies, waits for them, and re-layouts  55.1 us (16%)
  other arithmetic  39.3 us (11%)
  starting transfers between devices  23 us (7%)
  matrix products  20 us (6%)
  between operations  14.5 us (4%)
    ppermute x5, waiting for transfers between devices, collect(): lax.ppermute(line, axis, [(d, (d - have) % ways) for d in range(ways)])  188 us
    scatter-add x6, other arithmetic, per_device(): spread = spread.at[:, neighbours[:, entry]].add(edges)  25.5 us
    unnamed x165, local copies, waits for them, and re-layouts  18.4 us
    ppermute x2, starting transfers between devices, padded(): after = lax.ppermute(leading, axis, down)  16.1 us
    dot_general x1, matrix products, mlp_back(): jnp.einsum('brh,wh->brw', grad_pre, up_mat, preferred_element_type=jnp.fl...  11.5 us
    gather x6, local copies, waits for them, and re-layouts, per_device(): near = extended[:, neighbours[:, entry]].astype(jnp.float32)  9.1 us
    convert_element_type x6, local copies, waits for them, and re-layouts, per_device(): near = extended[:, neighbours[:, entry]].astype(jnp.float32)  8.73 us
  transfers between devices with their start and end apart: 10, of which 5 were waited for; matrix products, arithmetic and copies ran while one was open for 18% of the time, Pallas kernels for 0%

profile of v1, /device:TPU:0, one launch (start us, length us, event | category | flops | bytes accessed | tf_op | source)
XLA Modules:
  0.0 343.3 jit_solution(8593800781094205047)
XLA Ops:
  7.3 6.5 %collective-permute-start.2 = (bf16[48,2048]{1,0:T(8,128)(2,1)}, bf16[48,2048]{1,0:T(8,128)(2,1)S(1)}, u32[]{:S(2)}, u32[]{:S(2)}) collective-permute-start(bf16[48,2048]{1,0:T(8,128)(2,1)} %param.21), channel_id=1, source_target_pairs={{0,31},{1,0},{2,1},{3,2},{4,3},{5,4},{6,5},{7,6},{8,7},{9,8},{10,9... | collective-permute-start | bytes 589832 | tf_op jit(solution)/shard_map/ppermute | solution.py:14
  18.2 5.4 %collective-permute-start.1 = (bf16[1,1,32,1536]{3,2,1,0:T(8,128)(2,1)S(1)}, bf16[1,1,32,1536]{3,2,1,0:T(8,128)(2,1)S(1)}, u32[]{:S(2)}, u32[]{:S(2)}) collective-permute-start(bf16[1,1,32,1536]{3,2,1,0:T(8,128)(2,1)S(1)} %bitcast.177), channel_id=1, source_target_pairs={{1,0},{2,1},{3,2},{4,3},{5,4},{6,5},{7,6},{8,7},{9,8},{10,9},{11,1... | collective-permute-start | bytes 294920 | tf_op jit(solution)/shard_map/ppermute | solution.py:29
  24.6 3.2 gather_fusion
  31.8 6.9 %collective-permute-done.3 = bf16[96,2048]{1,0:T(8,128)(2,1)S(1)} collective-permute-done((bf16[96,2048]{1,0:T(8,128)(2,1)S(1)}, bf16[96,2048]{1,0:T(8,128)(2,1)S(1)}, u32[]{:S(2)}, u32[]{:S(2)}) %collective-permute-start.3) | collective-permute-done | bytes 393248 | tf_op jit(solution)/shard_map/ppermute | solution.py:14
  41.5 22.8 %collective-permute-done.4 = bf16[192,2048]{1,0:T(8,128)(2,1)S(1)} collective-permute-done((bf16[192,2048]{1,0:T(8,128)(2,1)S(1)}, bf16[192,2048]{1,0:T(8,128)(2,1)S(1)}, u32[]{:S(2)}, u32[]{:S(2)}) %collective-permute-start.4) | collective-permute-done | bytes 786464 | tf_op jit(solution)/shard_map/ppermute | solution.py:14
  75.7 42.6 %collective-permute-done.5 = bf16[384,2048]{1,0:T(8,128)(2,1)} collective-permute-done((bf16[384,2048]{1,0:T(8,128)(2,1)}, bf16[384,2048]{1,0:T(8,128)(2,1)}, u32[]{:S(2)}, u32[]{:S(2)}) %collective-permute-start.5) | collective-permute-done | bytes 1572896 | tf_op jit(solution)/shard_map/ppermute | solution.py:14
  118.3 3.5 %constant_dynamic-update-slice_fusion = (bf16[768,2048]{1,0:T(8,128)(2,1)}, bf16[3072,2048]{1,0:T(8,128)(2,1)}) fusion(bf16[768,2048]{1,0:T(8,128)(2,1)} %get-tuple-element.25, bf16[384,2048]{1,0:T(8,128)(2,1)} %collective-permute-done.5, bf16[3072,2048]{1,0:T(8,128)(2,1)} %get-tuple-element.26), kind=kLoop, calls=%fused_computation.151 | loop fusion | bytes 4718592 | tf_op jit(solution)/shard_map/concatenate | solution.py:13
  127.3 2.1 copy.92
  131.0 2.0 copy.94
  134.7 2.1 copy.96
  142.4 115.9 %collective-permute-done.6 = bf16[768,2048]{1,0:T(8,128)(2,1)} collective-permute-done((bf16[768,2048]{1,0:T(8,128)(2,1)}, bf16[768,2048]{1,0:T(8,128)(2,1)}, u32[]{:S(2)}, u32[]{:S(2)}) %collective-permute-start.6) | collective-permute-done | bytes 3145760 | tf_op jit(solution)/shard_map/ppermute | solution.py:14
  258.3 4.1 %constant_dynamic-update-slice_fusion.11 = bf16[3072,2048]{1,0:T(8,128)(2,1)} fusion(bf16[3072,2048]{1,0:T(8,128)(2,1)} %get-tuple-element.20, bf16[768,2048]{1,0:T(8,128)(2,1)} %collective-permute-done.6), kind=kLoop, calls=%fused_computation.162 | loop fusion | bytes 6291456
  265.6 2.8 constant_dynamic-update-slice_fusion.6
  268.4 4.0 %constant_dynamic-update-slice_fusion.5 = bf16[3072,2048]{1,0:T(8,128)(2,1)} fusion(bf16[3072,2048]{1,0:T(8,128)(2,1)} %constant_dynamic-update-slice_fusion.6, bf16[768,2048]{1,0:T(8,128)(2,1)} %collective-permute-done.6), kind=kLoop, calls=%fused_computation.156 | loop fusion | bytes 6291456 | tf_op jit(solution)/shard_map/jit(_roll_dynamic)/concatenate | solution.py:18
  272.5 5.5 %fusion.67 = f32[128,2048]{0,1:T(8,128)S(1)} fusion(bf16[1536,2048]{1,0:T(8,128)(2,1)} %all-gather.2.cloned.1.call-done, bf16[1,128,1536]{2,1,0:T(8,128)(2,1)S(1)} %add_convert_fusion, f32[1536]{0:T(1024)S(1)} %copy-done.30, f32[128]{0:T(128)S(1)} %add_rsqrt_fusion), kind=kOutput, calls=%fused_computation.92 | convolution fusion | flops 806092800 | bytes 7739904 | tf_op jit(solution)/shard_map/brw,wh->brh/dot_general | solution.py:58
  278.0 11.5 %fusion.26 = (f32[128]{0:T(128)S(1)}, f32[128,1536]{1,0:T(8,128)S(1)}) fusion(bf16[1,128,1536]{2,1,0:T(8,128)(2,1)S(1)} %add_convert_fusion, f32[1536]{0:T(1024)S(1)} %copy-done.30, bf16[1536,2048]{1,0:T(8,128)(2,1)} %all-gather.2.cloned.1.call-done, bf16[3072,2048]{1,0:T(8,128)(2,1)} %constant_dynamic-update-slice_fusion.5, s32[]{:T(128)S(6)} %select_n.78, ...), kind=kOutput, calls=%fused_computation.39 | convolution fusion | flops 1613758336 | bytes 15211012 | tf_op jit(solution)/shard_map/brh,wh->brw/dot_general | solution.py:64
  291.7 3.2 scatter_custom_fusion
  294.9 4.6 %scatter_custom_fusion.1 = f32[193,1536]{1,0:T(8,128)} fusion(f32[193,1536]{1,0:T(8,128)} %scatter_custom_fusion, s32[128]{0:T(128)} %copy-done.71, f32[1,128,1536]{2,1,0:T(8,128)S(1)} %copy.115, f32[1,128,1536]{2,1,0:T(8,128)S(1)} %copy.114, f32[128]{0:T(128)} %get-tuple-element.50, f32[128]{0:T(128)} %get-tuple-element.16, f32[128]{0:T(128)} %get-tuple-element.71), kind=kCustom, calls=%fused_computation.58 | custom fusion | flops 983040 | bytes 2760192 | tf_op jit(solution)/shard_map/scatter-add | solution.py:145
  299.5 4.4 %scatter_custom_fusion.2 = f32[193,1536]{1,0:T(8,128)} fusion(f32[193,1536]{1,0:T(8,128)} %scatter_custom_fusion.1, s32[128]{0:T(128)} %copy-done.70, f32[1,128,1536]{2,1,0:T(8,128)S(1)} %copy.115, f32[1,128,1536]{2,1,0:T(8,128)S(1)} %copy.114, f32[128]{0:T(128)S(1)} %copy-done.65, f32[128]{0:T(128)S(1)} %copy-done.53, f32[128]{0:T(128)S(1)} %copy-done.55), kind=kCustom, calls=%fused_computation.56 | custom fusion | flops 983040 | bytes 2760192 | tf_op jit(solution)/shard_map/scatter-add | solution.py:145
  303.9 4.4 %scatter_custom_fusion.3 = f32[193,1536]{1,0:T(8,128)} fusion(f32[193,1536]{1,0:T(8,128)} %scatter_custom_fusion.2, s32[128]{0:T(128)} %copy-done.69, f32[1,128,1536]{2,1,0:T(8,128)S(1)} %copy.115, f32[1,128,1536]{2,1,0:T(8,128)S(1)} %copy.114, f32[128]{0:T(128)S(1)} %copy-done.63, f32[128]{0:T(128)S(1)} %copy-done.49, f32[128]{0:T(128)S(1)} %copy-done.51), kind=kCustom, calls=%fused_computation.54 | custom fusion | flops 983040 | bytes 2760192 | tf_op jit(solution)/shard_map/scatter-add | solution.py:145
  308.4 4.4 %scatter_custom_fusion.4 = f32[193,1536]{1,0:T(8,128)} fusion(f32[193,1536]{1,0:T(8,128)} %scatter_custom_fusion.3, s32[128]{0:T(128)} %copy-done.68, f32[1,128,1536]{2,1,0:T(8,128)S(1)} %copy.115, f32[1,128,1536]{2,1,0:T(8,128)S(1)} %copy.114, f32[128]{0:T(128)S(1)} %copy-done.61, f32[128]{0:T(128)S(1)} %copy-done.45, f32[128]{0:T(128)S(1)} %copy-done.47), kind=kCustom, calls=%fused_computation.52 | custom fusion | flops 983040 | bytes 2760192 | tf_op jit(solution)/shard_map/scatter-add | solution.py:145
  312.8 4.4 %scatter_custom_fusion.5 = f32[193,1536]{1,0:T(8,128)} fusion(f32[193,1536]{1,0:T(8,128)} %scatter_custom_fusion.4, s32[128]{0:T(128)} %copy-done.67, f32[1,128,1536]{2,1,0:T(8,128)S(1)} %copy.115, f32[1,128,1536]{2,1,0:T(8,128)S(1)} %copy.114, f32[128]{0:T(128)S(1)} %copy-done.59, f32[128]{0:T(128)S(1)} %copy-done.41, f32[128]{0:T(128)S(1)} %copy-done.43), kind=kCustom, calls=%fused_computation.50 | custom fusion | flops 983040 | bytes 2760192 | tf_op jit(solution)/shard_map/scatter-add | solution.py:145
  320.0 10.7 %collective-permute-start.8 = (bf16[1,1,32,1536]{3,2,1,0:T(8,128)(2,1)S(1)}, bf16[1,1,32,1536]{3,2,1,0:T(8,128)(2,1)S(1)}, u32[]{:S(2)}, u32[]{:S(2)}) collective-permute-start(bf16[1,1,32,1536]{3,2,1,0:T(8,128)(2,1)S(1)} %bitcast.172), channel_id=1, source_target_pairs={{1,0},{2,1},{3,2},{4,3},{5,4},{6,5},{7,6},{8,7},{9,8},{10,9},{11,1... | collective-permute-start | bytes 294920 | tf_op jit(solution)/shard_map/ppermute | solution.py:29
  330.7 2.2 collective-permute-done.7
  (245 shorter events, 49.3 us)
Async XLA Ops:
  6.5 18.0 %copy-start = (f32[1024]{0:T(1024)S(1)}, f32[1024]{0:T(1024)}, u32[]{:S(2)}) copy-start(f32[1024]{0:T(1024)} %param.18) | copy-start | bytes 12292
  6.5 265.9 %all-gather.2.cloned.1.call-start = ((), (), s32[]{:S(2)}) async-start(), calls=%async_computation | async-start | bytes 6488064 | tf_op jit(solution)/shard_map/all_gather | solution.py:121
  7.3 21.1 %collective-permute-start.2 = (bf16[48,2048]{1,0:T(8,128)(2,1)}, bf16[48,2048]{1,0:T(8,128)(2,1)S(1)}, u32[]{:S(2)}, u32[]{:S(2)}) collective-permute-start(bf16[48,2048]{1,0:T(8,128)(2,1)} %param.21), channel_id=1, source_target_pairs={{0,31},{1,0},{2,1},{3,2},{4,3},{5,4},{6,5},{7,6},{8,7},{9,8},{10,9... | collective-permute-start | bytes 589832 | tf_op jit(solution)/shard_map/ppermute | solution.py:14
  16.3 49.6 %collective-permute-start = (bf16[1,1,32,1536]{3,2,1,0:T(8,128)(2,1)S(1)}, bf16[1,1,32,1536]{3,2,1,0:T(8,128)(2,1)S(1)}, u32[]{:S(2)}, u32[]{:S(2)}) collective-permute-start(bf16[1,1,32,1536]{3,2,1,0:T(8,128)(2,1)S(1)} %bitcast.175), channel_id=1, source_target_pairs={{0,1},{1,2},{2,3},{3,4},{4,5},{5,6},{6,7},{7,8},{8,9},{9,10},{10,1... | collective-permute-start | bytes 294920 | tf_op jit(solution)/shard_map/ppermute | solution.py:28
  18.2 47.8 %collective-permute-start.1 = (bf16[1,1,32,1536]{3,2,1,0:T(8,128)(2,1)S(1)}, bf16[1,1,32,1536]{3,2,1,0:T(8,128)(2,1)S(1)}, u32[]{:S(2)}, u32[]{:S(2)}) collective-permute-start(bf16[1,1,32,1536]{3,2,1,0:T(8,128)(2,1)S(1)} %bitcast.177), channel_id=1, source_target_pairs={{1,0},{2,1},{3,2},{4,3},{5,4},{6,5},{7,6},{8,7},{9,8},{10,9},{11,1... | collective-permute-start | bytes 294920 | tf_op jit(solution)/shard_map/ppermute | solution.py:29
  27.8 11.1 %copy-start.69 = (s32[128]{0:T(128)}, s32[128]{0:T(128)S(1)}, u32[]{:S(2)}) copy-start(s32[128]{0:T(128)S(1)} %get-tuple-element.54) | copy-start | bytes 1540
  27.9 37.8 %copy-start.67 = (s32[128]{0:T(128)}, s32[128]{0:T(128)S(1)}, u32[]{:S(2)}) copy-start(s32[128]{0:T(128)S(1)} %get-tuple-element.57) | copy-start | bytes 1540
  27.9 37.8 %copy-start.68 = (s32[128]{0:T(128)}, s32[128]{0:T(128)S(1)}, u32[]{:S(2)}) copy-start(s32[128]{0:T(128)S(1)} %get-tuple-element.58) | copy-start | bytes 1540
  28.4 37.2 %copy-start.12 = (bf16[48,2048]{1,0:T(8,128)(2,1)}, bf16[48,2048]{1,0:T(8,128)(2,1)S(1)}, u32[]{:S(2)}) copy-start(bf16[48,2048]{1,0:T(8,128)(2,1)S(1)} %collective-permute-done.2) | copy-start | bytes 589828
  28.5 10.3 %collective-permute-start.3 = (bf16[96,2048]{1,0:T(8,128)(2,1)S(1)}, bf16[96,2048]{1,0:T(8,128)(2,1)S(1)}, u32[]{:S(2)}, u32[]{:S(2)}) collective-permute-start(bf16[96,2048]{1,0:T(8,128)(2,1)S(1)} %pad_maximum_fusion.9), channel_id=1, source_target_pairs={{0,30},{1,31},{2,0},{3,1},{4,2},{5,3},{6,4},{7,5},{8,6},{9,7},{10,... | collective-permute-start | bytes 1179656 | tf_op jit(solution)/shard_map/ppermute | solution.py:14
  29.2 36.5 %copy-start.22 = (bf16[32,32]{0,1:T(8,128)(2,1)}, bf16[32,32]{0,1:T(8,128)(2,1)S(1)}, u32[]{:S(2)}) copy-start(bf16[32,32]{0,1:T(8,128)(2,1)S(1)} %neg.59) | copy-start | bytes 6148
  29.3 36.4 %copy-start.24 = (bf16[32,32]{0,1:T(8,128)(2,1)}, bf16[32,32]{0,1:T(8,128)(2,1)S(1)}, u32[]{:S(2)}) copy-start(bf16[32,32]{0,1:T(8,128)(2,1)S(1)} %copy.102) | copy-start | bytes 6148
  29.4 9.4 %copy-start.18 = (bf16[32,32]{0,1:T(8,128)(2,1)}, bf16[32,32]{0,1:T(8,128)(2,1)S(1)}, u32[]{:S(2)}) copy-start(bf16[32,32]{0,1:T(8,128)(2,1)S(1)} %copy.99) | copy-start | bytes 6148
  38.8 26.9 %copy-start.7 = (bf16[96,2048]{1,0:T(8,128)(2,1)}, bf16[96,2048]{1,0:T(8,128)(2,1)S(1)}, u32[]{:S(2)}) copy-start(bf16[96,2048]{1,0:T(8,128)(2,1)S(1)} %collective-permute-done.3) | copy-start | bytes 1179652
  38.8 25.4 %collective-permute-start.4 = (bf16[192,2048]{1,0:T(8,128)(2,1)S(1)}, bf16[192,2048]{1,0:T(8,128)(2,1)S(1)}, u32[]{:S(2)}, u32[]{:S(2)}) collective-permute-start(bf16[192,2048]{1,0:T(8,128)(2,1)S(1)} %pad_maximum_fusion.7), channel_id=1, source_target_pairs={{0,28},{1,29},{2,30},{3,31},{4,0},{5,1},{6,2},{7,3},{8,4},{9,5},{1... | collective-permute-start | bytes 2359304 | tf_op jit(solution)/shard_map/ppermute | solution.py:14
  64.3 10.1 %copy-start.5 = (bf16[192,2048]{1,0:T(8,128)(2,1)}, bf16[192,2048]{1,0:T(8,128)(2,1)S(1)}, u32[]{:S(2)}) copy-start(bf16[192,2048]{1,0:T(8,128)(2,1)S(1)} %collective-permute-done.4) | copy-start | bytes 2359300
  65.7 52.7 %collective-permute-start.5 = (bf16[384,2048]{1,0:T(8,128)(2,1)}, bf16[384,2048]{1,0:T(8,128)(2,1)}, u32[]{:S(2)}, u32[]{:S(2)}) collective-permute-start(bf16[384,2048]{1,0:T(8,128)(2,1)} %pad_maximum_fusion), channel_id=1, source_target_pairs={{0,24},{1,25},{2,26},{3,27},{4,28},{5,29},{6,30},{7,31},{8,0},{9,1... | collective-permute-start | bytes 4718600 | tf_op jit(solution)/shard_map/ppermute | solution.py:14
  121.9 136.5 %collective-permute-start.6 = (bf16[768,2048]{1,0:T(8,128)(2,1)}, bf16[768,2048]{1,0:T(8,128)(2,1)}, u32[]{:S(2)}, u32[]{:S(2)}) collective-permute-start(bf16[768,2048]{1,0:T(8,128)(2,1)} %get-tuple-element.19), channel_id=1, source_target_pairs={{0,16},{1,17},{2,18},{3,19},{4,20},{5,21},{6,22},{7,23},{8,24},{9,... | collective-permute-start | bytes 9437192 | tf_op jit(solution)/shard_map/ppermute | solution.py:14
  278.0 12.2 %copy-start.20 = (bf16[32,32]{0,1:T(8,128)(2,1)S(1)}, bf16[32,32]{0,1:T(8,128)(2,1)}, u32[]{:S(2)}) copy-start(bf16[32,32]{0,1:T(8,128)(2,1)} %copy-done.18) | copy-start | bytes 6148
  278.0 12.2 %copy-start.27 = (bf16[32,32]{0,1:T(8,128)(2,1)S(1)}, bf16[32,32]{0,1:T(8,128)(2,1)}, u32[]{:S(2)}) copy-start(bf16[32,32]{0,1:T(8,128)(2,1)} %neg.58) | copy-start | bytes 6148
  278.0 12.2 %copy-start.29 = (bf16[32,32]{0,1:T(8,128)(2,1)S(1)}, bf16[32,32]{0,1:T(8,128)(2,1)}, u32[]{:S(2)}) copy-start(bf16[32,32]{0,1:T(8,128)(2,1)} %copy.98) | copy-start | bytes 6148
  294.9 9.0 %copy-start.63 = (f32[128]{0:T(128)S(1)}, f32[128]{0:T(128)}, u32[]{:S(2)}) copy-start(f32[128]{0:T(128)} %get-tuple-element.48) | copy-start | bytes 1540
  319.9 13.1 %collective-permute-start.7 = (bf16[1,1,32,1536]{3,2,1,0:T(8,128)(2,1)S(1)}, bf16[1,1,32,1536]{3,2,1,0:T(8,128)(2,1)S(1)}, u32[]{:S(2)}, u32[]{:S(2)}) collective-permute-start(bf16[1,1,32,1536]{3,2,1,0:T(8,128)(2,1)S(1)} %bitcast.173), channel_id=1, source_target_pairs={{0,1},{1,2},{2,3},{3,4},{4,5},{5,6},{6,7},{7,8},{8,9},{9,10},{10,1... | collective-permute-start | bytes 294920 | tf_op jit(solution)/shard_map/ppermute | solution.py:28
  320.0 13.0 %collective-permute-start.8 = (bf16[1,1,32,1536]{3,2,1,0:T(8,128)(2,1)S(1)}, bf16[1,1,32,1536]{3,2,1,0:T(8,128)(2,1)S(1)}, u32[]{:S(2)}, u32[]{:S(2)}) collective-permute-start(bf16[1,1,32,1536]{3,2,1,0:T(8,128)(2,1)S(1)} %bitcast.172), channel_id=1, source_target_pairs={{1,0},{2,1},{3,2},{4,3},{5,4},{6,5},{7,6},{8,7},{9,8},{10,9},{11,1... | collective-permute-start | bytes 294920 | tf_op jit(solution)/shard_map/ppermute | solution.py:29
  (61 other events, 218.6 us)
Sparse Core Ops, SparseCore 0:
  10.2 99.5 all-gather.1
